TPU v7x, 32 devices: a whole 2x2x4 slice. The times are simulated.
32 devices in a mesh: wide: 8 (over z, x), narrow: 4 (over y, core).
Axes of the slice: x: 2, y: 2, z: 4, core: 2. Of those that a mesh axis runs over, the one named last changes fastest.
Arguments:
- tokens: bfloat16 [32768, 768], P(('wide', 'narrow')), may hold values from -6 to 6
- norm1_gain: bfloat16 [768], P(('wide', 'narrow')), may hold values from 0.25 to 1.75
- norm1_bias: bfloat16 [768], P(('wide', 'narrow')), may hold values from -2.5 to 2.5
- qkv_weight: bfloat16 [768, 2304], P(('wide', 'narrow')), may hold values from -0.21875 to 0.21875
- qkv_bias: bfloat16 [1536], P(('wide', 'narrow')), may hold values from -2.5 to 2.5
- out_weight: bfloat16 [768, 768], P(('wide', 'narrow')), may hold values from -9 to 9
- out_bias: bfloat16 [768], P(('wide', 'narrow')), may hold values from -12 to 12
- norm2_gain: bfloat16 [768], P(('wide', 'narrow')), may hold values from 0.25 to 1.75
- norm2_bias: bfloat16 [768], P(('wide', 'narrow')), may hold values from -2.5 to 2.5
- fc_weight: bfloat16 [768, 3072], P(('wide', 'narrow')), may hold values from -0.21875 to 0.21875
- fc_bias: bfloat16 [3072], P(('wide', 'narrow')), may hold values from -3 to 3
- proj_weight: bfloat16 [3072, 768], P(('wide', 'narrow')), may hold values from -2.5 to 2.5
- proj_bias: bfloat16 [768], P(('wide', 'narrow')), may hold values from -12 to 12
- seq_lengths: int32 [32], P(('wide', 'narrow')), may hold values from 64 to 1024, as said below
- out_cotangent: bfloat16 [32768, 768], P(('wide', 'narrow')), may hold values from -6 to 6
Outputs:
- layer_out: bfloat16 [32768, 768], P(('wide', 'narrow'))
- input_grad: bfloat16 [32768, 768], P(('wide', 'narrow'))
- norm1_gain_grad: float32 [768], P(('wide', 'narrow'))
- norm1_bias_grad: float32 [768], P(('wide', 'narrow'))
- qkv_weight_grad: float32 [768, 2304], P(('wide', 'narrow'))
- qkv_bias_grad: float32 [1536], P(('wide', 'narrow'))
- out_weight_grad: float32 [768, 768], P(('wide', 'narrow'))
- out_bias_grad: float32 [768], P(('wide', 'narrow'))
- norm2_gain_grad: float32 [768], P(('wide', 'narrow'))
- norm2_bias_grad: float32 [768], P(('wide', 'narrow'))
- fc_weight_grad: float32 [768, 3072], P(('wide', 'narrow'))
- fc_bias_grad: float32 [3072], P(('wide', 'narrow'))
- proj_weight_grad: float32 [3072, 768], P(('wide', 'narrow'))
- proj_bias_grad: float32 [768], P(('wide', 'narrow'))
Inputs may be any that keep to these rules, and one draw needn't show every extreme that they name: Each slot holds one sequence of seq_lengths tokens from its first position on; the rest of the slot is padding. Some slot is full in every draw.
All inputs are finite; a program needn't handle non-finite values.
Results may differ from a plain program's by a relative error of at most 0.013.
Values may be sent and summed in bfloat16 or wider, within the bound.
No kernel may reach another device: no remote copies, remote signals or barrier semaphores. Data moves between devices by JAX's collectives and lax.ppermute only.
A program may use at most 256 MiB of HBM per device.

v0:
```python
import math
import jax
import jax.numpy as jnp
from jax import lax
from jax.sharding import PartitionSpec as P

D = 768
H = 12
HD = 64
branch_scale = 1.0 / math.sqrt(48.0)
norm_epsilon = 1e-05
masked_value = -1e30


def layer_norm(values_in, gain_vec, shift_vec):
    row_mean = jnp.mean(values_in, axis=-1, keepdims=True)
    centred = values_in - row_mean
    row_var = jnp.mean(centred * centred, axis=-1, keepdims=True)
    return centred * lax.rsqrt(row_var + norm_epsilon) * gain_vec + shift_vec


def gelu_tanh(pre_act):
    inner = 0.7978845608028654 * (pre_act + 0.044715 * pre_act * pre_act * pre_act)
    return 0.5 * pre_act * (1.0 + jnp.tanh(inner))


def product(left, right):
    return jnp.dot(left, right, preferred_element_type=jnp.float32)


def left_product(left, right):
    return lax.dot_general(
        left, right, (((0,), (0,)), ((), ())), preferred_element_type=jnp.float32
    )


def right_product(left, right):
    return lax.dot_general(
        left, right, (((1,), (1,)), ((), ())), preferred_element_type=jnp.float32
    )


def split_heads(packed_slot):
    slot_size = packed_slot.shape[0]
    query_rows = packed_slot[:, :D].reshape(slot_size, H, HD)
    key_rows = packed_slot[:, D : 2 * D].reshape(slot_size, H, HD)
    value_rows = packed_slot[:, 2 * D :].reshape(slot_size, H, HD)
    return (query_rows, key_rows, value_rows)


def block_scores(query_block, key_block, block_start):
    score_scale = 1.0 / math.sqrt(HD)
    raw_scores = (
        jnp.einsum("qhd,khd->hqk", query_block, key_block, preferred_element_type=jnp.float32)
        * score_scale
    )
    row_place = block_start + jnp.arange(query_block.shape[0])
    col_place = jnp.arange(key_block.shape[0])
    causal = col_place[None, :] <= row_place[:, None]
    return (jnp.where(causal[None], raw_scores, masked_value), causal)


def forward_block(query_block, key_block, value_block, block_start):
    scores, causal = block_scores(query_block, key_block, block_start)
    row_max = jnp.max(scores, axis=-1, keepdims=True)
    shifted = jnp.exp(scores - row_max)
    row_total = jnp.sum(shifted, axis=-1, keepdims=True)
    soft_probs = (shifted / row_total).astype(jnp.bfloat16)
    mixed_rows = jnp.einsum(
        "hqk,khd->qhd", soft_probs, value_block, preferred_element_type=jnp.float32
    )
    return (mixed_rows, (row_max + jnp.log(row_total))[:, :, 0])


def slot_forward(item):
    packed_slot, seq_length = item
    query_rows, key_rows, value_rows = split_heads(packed_slot)
    slot_size = packed_slot.shape[0]
    block_rows = min(512, slot_size)
    mixed_parts = []
    stats_parts = []
    for block_index in range(slot_size // block_rows):
        block_start = block_index * block_rows
        block_end = block_start + block_rows
        query_block = query_rows[block_start:block_end]
        key_block = key_rows[:block_end]
        value_block = value_rows[:block_end]

        def compute_block():
            return forward_block(query_block, key_block, value_block, block_start)

        mixed_block, block_stats = compute_block()
        mixed_parts.append(mixed_block)
        stats_parts.append(block_stats)
    mixed_rows = jnp.concatenate(mixed_parts, 0)
    valid_rows = (jnp.arange(slot_size) < seq_length).astype(jnp.float32)
    mixed_rows = mixed_rows * valid_rows[:, None, None]
    return (mixed_rows.reshape(slot_size, D), jnp.concatenate(stats_parts, 1))


def slot_backward(item):
    packed_slot, grad_slot, slot_stats, seq_length = item
    query_rows, key_rows, value_rows = split_heads(packed_slot)
    slot_size = packed_slot.shape[0]
    grad_rows = grad_slot.reshape(slot_size, H, HD)
    score_scale = 1.0 / math.sqrt(HD)
    block_rows = min(512, slot_size)
    query_parts = []
    key_grad = jnp.zeros((slot_size, H, HD), jnp.float32)
    value_grad = jnp.zeros((slot_size, H, HD), jnp.float32)
    for block_index in range(slot_size // block_rows):
        block_start = block_index * block_rows
        block_end = block_start + block_rows
        query_block = query_rows[block_start:block_end]
        key_block = key_rows[:block_end]
        value_block = value_rows[:block_end]
        grad_block = grad_rows[block_start:block_end]
        stats_block = slot_stats[:, block_start:block_end]

        def compute_block():
            scores, causal = block_scores(query_block, key_block, block_start)
            soft_probs = jnp.where(causal[None], jnp.exp(scores - stats_block[:, :, None]), 0.0)
            low_probs = soft_probs.astype(jnp.bfloat16)
            value_part = jnp.einsum(
                "hqk,qhd->khd", low_probs, grad_block, preferred_element_type=jnp.float32
            )
            prob_grad = jnp.einsum(
                "qhd,khd->hqk", grad_block, value_block, preferred_element_type=jnp.float32
            )
            row_delta = jnp.sum(soft_probs * prob_grad, axis=-1, keepdims=True)
            score_grad = (soft_probs * (prob_grad - row_delta)).astype(jnp.bfloat16)
            query_part = (
                jnp.einsum(
                    "hqk,khd->qhd", score_grad, key_block, preferred_element_type=jnp.float32
                )
                * score_scale
            )
            key_part = (
                jnp.einsum(
                    "hqk,qhd->khd", score_grad, query_block, preferred_element_type=jnp.float32
                )
                * score_scale
            )
            return (query_part, key_part, value_part)

        query_part, key_part, value_part = compute_block()
        pad_rows = ((0, slot_size - block_end), (0, 0), (0, 0))
        key_grad = key_grad + jnp.pad(key_part, pad_rows)
        value_grad = value_grad + jnp.pad(value_part, pad_rows)
        query_parts.append(query_part)
    query_grad = jnp.concatenate(query_parts, 0)
    return jnp.concatenate(
        [
            query_grad.reshape(slot_size, D),
            key_grad.reshape(slot_size, D),
            value_grad.reshape(slot_size, D),
        ],
        axis=1,
    )


def local(
    tokens,
    norm1_gain,
    norm1_bias,
    qkv_weight,
    qkv_bias,
    out_weight,
    out_bias,
    norm2_gain,
    norm2_bias,
    fc_weight,
    fc_bias,
    proj_weight,
    proj_bias,
    seq_lengths,
    out_cotangent,
):
    attn_full = (
        lax.all_gather(norm1_gain, ("wide", "narrow"), axis=0, tiled=True),
        lax.all_gather(norm1_bias, ("wide", "narrow"), axis=0, tiled=True),
        lax.all_gather(qkv_weight, ("wide", "narrow"), axis=0, tiled=True),
        lax.all_gather(qkv_bias, ("wide", "narrow"), axis=0, tiled=True),
        lax.all_gather(out_weight, ("wide", "narrow"), axis=0, tiled=True),
        lax.all_gather(out_bias, ("wide", "narrow"), axis=0, tiled=True),
    )
    gain_one, shift_one, qkv_full, qkv_bias_full, out_full, out_bias_full = attn_full
    slot_count = seq_lengths.shape[0]
    slot_size = tokens.shape[0] // slot_count
    position = jnp.arange(slot_size)
    valid_rows = (position[None, :] < seq_lengths[:, None]).reshape(-1, 1).astype(jnp.float32)
    input_rows = tokens.astype(jnp.float32)
    gain_one_f = gain_one.astype(jnp.float32)
    shift_one_f = shift_one.astype(jnp.float32)
    norm_one = layer_norm(input_rows, gain_one_f, shift_one_f)
    low_one = norm_one.astype(jnp.bfloat16)
    bias_full = jnp.concatenate(
        [
            qkv_bias_full[:D].astype(jnp.float32),
            jnp.zeros((D,), jnp.float32),
            qkv_bias_full[D:].astype(jnp.float32),
        ]
    )
    packed = (product(low_one, qkv_full) + bias_full).astype(jnp.bfloat16)
    slot_packed = packed.reshape(slot_count, slot_size, 3 * D)
    mixed_all, stats_all = lax.map(slot_forward, (slot_packed, seq_lengths))
    low_mixed = mixed_all.reshape(-1, D).astype(jnp.bfloat16)
    branch = product(low_mixed, out_full) + out_bias_full.astype(jnp.float32)
    middle = input_rows + branch_scale * branch
    mlp_full = (
        lax.all_gather(norm2_gain, ("wide", "narrow"), axis=0, tiled=True),
        lax.all_gather(norm2_bias, ("wide", "narrow"), axis=0, tiled=True),
        lax.all_gather(fc_weight, ("wide", "narrow"), axis=0, tiled=True),
        lax.all_gather(fc_bias, ("wide", "narrow"), axis=0, tiled=True),
        lax.all_gather(proj_weight, ("wide", "narrow"), axis=0, tiled=True),
        lax.all_gather(proj_bias, ("wide", "narrow"), axis=0, tiled=True),
    )
    gain_two, shift_two, fc_full, fc_bias_full, proj_full, proj_bias_full = mlp_full
    gain_two_f = gain_two.astype(jnp.float32)
    shift_two_f = shift_two.astype(jnp.float32)
    norm_two = layer_norm(middle, gain_two_f, shift_two_f)
    low_two = norm_two.astype(jnp.bfloat16)
    hidden = product(low_two, fc_full) + fc_bias_full.astype(jnp.float32)
    low_active = gelu_tanh(hidden).astype(jnp.bfloat16)
    second = product(low_active, proj_full) + proj_bias_full.astype(jnp.float32)
    layer_out = (middle + branch_scale * second).astype(jnp.bfloat16)
    mlp_back = (
        lax.all_gather(norm2_gain, ("wide", "narrow"), axis=0, tiled=True),
        lax.all_gather(norm2_bias, ("wide", "narrow"), axis=0, tiled=True),
        lax.all_gather(fc_weight, ("wide", "narrow"), axis=0, tiled=True),
        lax.all_gather(fc_bias, ("wide", "narrow"), axis=0, tiled=True),
        lax.all_gather(proj_weight, ("wide", "narrow"), axis=0, tiled=True),
        lax.all_gather(proj_bias, ("wide", "narrow"), axis=0, tiled=True),
    )
    fc_back = mlp_back[2]
    proj_back = mlp_back[4]
    cotangent = out_cotangent.astype(jnp.float32) * valid_rows
    grad_second = (branch_scale * cotangent).astype(jnp.bfloat16)
    proj_weight_term = left_product(low_active, grad_second)
    proj_bias_term = jnp.sum(grad_second.astype(jnp.float32), axis=0)
    grad_active = right_product(grad_second, proj_back)
    unused_value, gelu_pull = jax.vjp(gelu_tanh, hidden)
    grad_hidden = gelu_pull(grad_active)[0].astype(jnp.bfloat16)
    fc_weight_term = left_product(low_two, grad_hidden)
    fc_bias_term = jnp.sum(grad_hidden.astype(jnp.float32), axis=0)
    grad_norm_two = right_product(grad_hidden, fc_back)
    unused_norm, norm_two_pull = jax.vjp(layer_norm, middle, gain_two_f, shift_two_f)
    middle_part, gain_two_term, shift_two_term = norm_two_pull(grad_norm_two)
    grad_middle = cotangent + middle_part
    mlp_grads = (
        lax.psum_scatter(gain_two_term, ("wide", "narrow"), scatter_dimension=0, tiled=True),
        lax.psum_scatter(shift_two_term, ("wide", "narrow"), scatter_dimension=0, tiled=True),
        lax.psum_scatter(fc_weight_term, ("wide", "narrow"), scatter_dimension=0, tiled=True),
        lax.psum_scatter(fc_bias_term, ("wide", "narrow"), scatter_dimension=0, tiled=True),
        lax.psum_scatter(proj_weight_term, ("wide", "narrow"), scatter_dimension=0, tiled=True),
        lax.psum_scatter(proj_bias_term, ("wide", "narrow"), scatter_dimension=0, tiled=True),
    )
    attn_back = (
        lax.all_gather(norm1_gain, ("wide", "narrow"), axis=0, tiled=True),
        lax.all_gather(norm1_bias, ("wide", "narrow"), axis=0, tiled=True),
        lax.all_gather(qkv_weight, ("wide", "narrow"), axis=0, tiled=True),
        lax.all_gather(qkv_bias, ("wide", "narrow"), axis=0, tiled=True),
        lax.all_gather(out_weight, ("wide", "narrow"), axis=0, tiled=True),
        lax.all_gather(out_bias, ("wide", "narrow"), axis=0, tiled=True),
    )
    qkv_back = attn_back[2]
    out_back = attn_back[4]
    grad_branch = (branch_scale * grad_middle).astype(jnp.bfloat16)
    out_weight_term = left_product(low_mixed, grad_branch)
    out_bias_term = jnp.sum(grad_branch.astype(jnp.float32), axis=0)
    grad_mixed = right_product(grad_branch, out_back).astype(jnp.bfloat16) * valid_rows.astype(
        jnp.bfloat16
    )
    grad_packed = lax.map(
        slot_backward,
        (slot_packed, grad_mixed.reshape(slot_count, slot_size, D), stats_all, seq_lengths),
    )
    low_grad_packed = grad_packed.reshape(-1, 3 * D).astype(jnp.bfloat16)
    qkv_weight_term = left_product(low_one, low_grad_packed)
    column_sums = jnp.sum(low_grad_packed.astype(jnp.float32), axis=0)
    qkv_bias_term = jnp.concatenate([column_sums[:D], column_sums[2 * D :]])
    grad_norm_one = right_product(low_grad_packed, qkv_back)
    unused_first, norm_one_pull = jax.vjp(layer_norm, input_rows, gain_one_f, shift_one_f)
    input_part, gain_one_term, shift_one_term = norm_one_pull(grad_norm_one)
    input_grad = (grad_middle + input_part).astype(jnp.bfloat16)
    attn_grads = (
        lax.psum_scatter(gain_one_term, ("wide", "narrow"), scatter_dimension=0, tiled=True),
        lax.psum_scatter(shift_one_term, ("wide", "narrow"), scatter_dimension=0, tiled=True),
        lax.psum_scatter(qkv_weight_term, ("wide", "narrow"), scatter_dimension=0, tiled=True),
        lax.psum_scatter(qkv_bias_term, ("wide", "narrow"), scatter_dimension=0, tiled=True),
        lax.psum_scatter(out_weight_term, ("wide", "narrow"), scatter_dimension=0, tiled=True),
        lax.psum_scatter(out_bias_term, ("wide", "narrow"), scatter_dimension=0, tiled=True),
    )
    return (
        layer_out,
        input_grad,
        attn_grads[0],
        attn_grads[1],
        attn_grads[2],
        attn_grads[3],
        attn_grads[4],
        attn_grads[5],
        mlp_grads[0],
        mlp_grads[1],
        mlp_grads[2],
        mlp_grads[3],
        mlp_grads[4],
        mlp_grads[5],
    )


def solution(mesh):
    placed = (
        P(("wide", "narrow"), None),
        P(("wide", "narrow")),
        P(("wide", "narrow")),
        P(("wide", "narrow"), None),
        P(("wide", "narrow")),
        P(("wide", "narrow"), None),
        P(("wide", "narrow")),
        P(("wide", "narrow")),
        P(("wide", "narrow")),
        P(("wide", "narrow"), None),
        P(("wide", "narrow")),
        P(("wide", "narrow"), None),
        P(("wide", "narrow")),
        P(("wide", "narrow")),
        P(("wide", "narrow"), None),
    )
    return jax.shard_map(
        local,
        mesh=mesh,
        in_specs=placed,
        out_specs=(
            P(("wide", "narrow"), None),
            P(("wide", "narrow"), None),
            P(("wide", "narrow")),
            P(("wide", "narrow")),
            P(("wide", "narrow"), None),
            P(("wide", "narrow")),
            P(("wide", "narrow"), None),
            P(("wide", "narrow")),
            P(("wide", "narrow")),
            P(("wide", "narrow")),
            P(("wide", "narrow"), None),
            P(("wide", "narrow")),
            P(("wide", "narrow"), None),
            P(("wide", "narrow")),
        ),
        check_vma=False,
    )
```

profile of v0, /device:TPU:0, one launch (start us, length us, event | category | flops | bytes accessed | tf_op | source)
XLA Modules:
  0.0 832.8 jit_solution(7919244227806289655)
XLA Ops:
  18.7 42.8 %all-reduce.19 = (bf16[768]{0:T(1024)(128)(2,1)S(1)}, bf16[1536]{0:T(1024)(128)(2,1)S(1)}, bf16[768]{0:T(1024)(128)(2,1)S(1)}, bf16[768]{0:T(1024)(128)(2,1)S(1)...) all-reduce(bf16[768]{0:T(1024)(128)(2,1)S(1)} %dynamic-update-slice, ...), channel_id=1, replica_groups=mesh['wide'=8,'narrow'=4] {'wide','narrow'}, use_global_device_ids=true, to_apply=%add.5 | all-reduce | flops 9216 | bytes 36864
  68.7 5.4 all-gather.5.cloned.1.call-done
  74.1 6.4 add_convert_fusion
  106.8 14.6 %fusion.2 = (f32[12,512]{1,0:T(8,128)S(1)}, f32[12,512,1024]{2,1,0:T(8,128)}) fusion(pred[512,1024]{1,0:T(8,128)(4,1)} %iota_compare_fusion, bf16[512,12,64]{0,2,1:T(8,128)(2,1)} %bitcast.76, bf16[1024,12,64]{0,2,1:T(8,128)(2,1)} %bitcast.72), kind=kOutput, calls=%fused_computation.11 | convolution fusion | flops 824174592 | bytes 28073984 | tf_op jit(solution)/shard_map/while/body/eval_jaxpr/qhd,khd->hqk/dot_general | solution.py:54
  121.4 13.4 %fusion = f32[12,512]{1,0:T(8,128)S(1)} fusion(f32[12,512,1024]{2,1,0:T(8,128)} %get-tuple-element.124, f32[12,512]{1,0:T(8,128)S(1)} %get-tuple-element.123, pred[512,1024]{1,0:T(8,128)(4,1)S(1)} %copy-done.11), kind=kLoop, calls=%fused_computation.6 | loop fusion | flops 25159680 | bytes 25739264 | tf_op jit(solution)/shard_map/while/body/eval_jaxpr/reduce_sum | solution.py:67
  134.9 8.1 fusion.17
  145.0 9.7 %fusion.12 = f32[12,64,512]{2,1,0:T(8,128)} fusion(bf16[1024,12,64]{0,2,1:T(8,128)(2,1)} %bitcast.86, f32[12,512,1024]{2,1,0:T(8,128)S(1)} %bitcast.69, f32[12,512]{1,0:T(8,128)S(1)} %fusion, f32[12,512]{1,0:T(8,128)S(1)} %get-tuple-element.123, pred[512,1024]{1,0:T(8,128)(4,1)S(1)} %copy-done.11), kind=kOutput, calls=%fused_computation.29 | convolution fusion | flops 836763648 | bytes 28884992 | tf_op jit(solution)/shard_map/while/body/eval_jaxpr/hqk,khd->qhd/dot_general | solution.py:69
  154.7 5.6 fusion.76
  163.3 32.1 %all-gather.9.cloned.1.call-done = bf16[768,3072]{1,0:T(8,128)(2,1)} async-done(((bf16[24,3072]{1,0:T(8,128)(2,1)}), bf16[768,3072]{1,0:T(8,128)(2,1)}) %all-gather.9.cloned.1.call-update) | async-done | bytes 4718608 | tf_op jit(solution)/shard_map/all_gather | solution.py:213
  195.4 11.0 %fusion.68 = f32[1024,3072]{1,0:T(8,128)} fusion(bf16[768,3072]{1,0:T(8,128)(2,1)} %all-gather.9.cloned.1.call-done, f32[1024,768]{0,1:T(8,128)} %get-tuple-element.128, f32[768]{0:T(1024)S(1)} %convert_element_type.145, f32[768]{0:T(1024)S(1)} %convert_element_type.144, f32[1024]{0:T(1024)S(1)} %fusion.47, f32[1024]{0:T(1024)S(1)} %broadcast_multiply_fusion), kind=kOutput, calls=%fused_computation.123 | convolution fusion | flops 4835770368 | bytes 20461568 | tf_op jit(solution)/shard_map/dot_general | solution.py:28
  206.4 54.2 %all-gather.11.cloned.1.call-done = bf16[3072,768]{1,0:T(8,128)(2,1)} async-done(((bf16[96,768]{1,0:T(8,128)(2,1)}), bf16[3072,768]{1,0:T(8,128)(2,1)}) %all-gather.11.cloned.1.call-update) | async-done | bytes 4718608 | tf_op jit(solution)/shard_map/all_gather | solution.py:215
  260.6 18.6 %convert_reduce_fusion = (f32[3072]{0:T(1024)}, bf16[1024,3072]{1,0:T(8,128)(2,1)S(1)}) fusion(f32[1024,3072]{1,0:T(8,128)} %fusion.68, f32[3072]{0:T(1024)S(1)} %copy-done.44, bf16[3072,768]{1,0:T(8,128)(2,1)} %all-gather.11.cloned.1.call-done, bf16[1024,768]{0,1:T(8,128)(2,1)S(1)} %copy.82, f32[1024]{0:T(1024)S(1)} %copy-done.32), kind=kOutput, calls=%fused_computation.18 | convolution fusion | flops 4919915520 | bytes 25194496 | tf_op jit(solution)/shard_map/dot_general | solution.py:38
  279.2 7.3 fusion.78
  302.8 7.8 fusion.35
  310.7 7.0 multiply_reduce_fusion.1
  317.8 10.2 %multiply_convert_fusion.1 = bf16[12,512,512]{1,2,0:T(8,128)(2,1)S(1)} fusion(f32[12,512,512]{1,2,0:T(8,128)} %get-tuple-element.130, f32[12,512]{1,0:T(8,128)S(1)} %get-tuple-element.129, f32[12,512]{1,0:T(8,128)S(1)} %copy-done.26, f32[12,512,512]{1,2,0:T(8,128)} %copy-done, pred[512,512]{0,1:T(8,128)(4,1)S(1)} %iota_compare_fusion.1), kind=kLoop, calls=%fused_computation.21 | loop fusion | flops 22020096 | bytes 31768576 | tf_op jit(solution)/shard_map/while/body/eval_jaxpr/convert_element_type | solution.py:131
  331.5 22.1 %multiply_reduce_fusion = (f32[12,512]{1,0:T(8,128)S(1)}, f32[12,512,1024]{2,1,0:T(8,128)}) fusion(f32[12,512]{1,0:T(8,128)S(1)} %log_add_fusion, f32[12,512,1024]{2,1,0:T(8,128)} %get-tuple-element.124, pred[512,1024]{1,0:T(8,128)(4,1)S(1)} %copy-done.12, bf16[512,12,64]{0,2,1:T(8,128)(2,1)S(1)} %bitcast.93, bf16[1024,12,64]{0,2,1:T(8,128)(2,1)S(1)} %bitcast.87), kind=kOutput, calls=%fused_computation.1 | convolution fusion | flops 843048960 | bytes 53264384 | tf_op jit(solution)/shard_map/while/body/eval_jaxpr/qhd,khd->hqk/dot_general | solution.py:127
  353.6 18.1 %multiply_convert_fusion = bf16[12,512,1024]{2,1,0:T(8,128)(2,1)S(1)} fusion(f32[12,512,1024]{2,1,0:T(8,128)} %get-tuple-element.132, f32[12,512]{1,0:T(8,128)S(1)} %get-tuple-element.131, f32[12,512]{1,0:T(8,128)S(1)} %log_add_fusion, f32[12,512,1024]{2,1,0:T(8,128)} %get-tuple-element.124, pred[512,1024]{1,0:T(8,128)(4,1)} %iota_compare_fusion), kind=kLoop, calls=%fused_computation | loop fusion | flops 44040192 | bytes 63488000 | tf_op jit(solution)/shard_map/while/body/eval_jaxpr/convert_element_type | solution.py:131
  371.7 6.2 fusion.38
  378.0 4.0 fusion.31
  382.0 4.6 fusion.39
  388.5 12.8 %fusion.30 = bf16[1024,12,64]{0,2,1:T(8,128)(2,1)S(1)} fusion(f32[512,12,64]{0,2,1:T(8,128)S(1)} %copy-done.56, bf16[512,12,64]{0,2,1:T(8,128)(2,1)S(1)} %bitcast.94, f32[12,512]{1,0:T(8,128)S(1)} %log_add_fusion, f32[12,512,1024]{2,1,0:T(8,128)} %get-tuple-element.124, pred[512,1024]{1,0:T(8,128)(4,1)S(1)} %copy-done.13), kind=kOutput, calls=%fused_computation.57 | convolution fusion | flops 838336512 | bytes 29646848 | tf_op jit(solution)/shard_map/while/body/eval_jaxpr/hqk,qhd->khd/dot_general | solution.py:124
  402.5 7.0 fusion.63
  410.9 14.1 %fusion.40 = f32[3072,768]{1,0:T(8,128)} fusion(bf16[1024,768]{0,1:T(8,128)(2,1)S(1)} %copy-done.8, f32[1024]{0:T(1024)S(1)} %copy-done.32, f32[1024,3072]{1,0:T(8,128)} %fusion.68, f32[3072]{0:T(1024)S(1)} %copy-done.44), kind=kOutput, calls=%fused_computation.83 | convolution fusion | flops 4866441216 | bytes 23609344 | tf_op jit(solution)/shard_map/dot_general | solution.py:32
  425.7 10.7 %fusion.67 = f32[768,3072]{1,0:T(8,128)} fusion(bf16[1024,3072]{1,0:T(8,128)(2,1)} %copy-done.55, f32[1024,768]{0,1:T(8,128)} %get-tuple-element.128, f32[768]{0:T(1024)S(1)} %copy-done.25, f32[768]{0:T(1024)S(1)} %convert_element_type.144, f32[1024]{0:T(1024)S(1)} %fusion.47, f32[1024]{0:T(1024)S(1)} %broadcast_multiply_fusion), kind=kOutput, calls=%fused_computation.122 | convolution fusion | flops 4835770368 | bytes 18888704 | tf_op jit(solution)/shard_map/dot_general | solution.py:32
  437.1 12.4 %add_convert_fusion.2 = bf16[1024,768]{0,1:T(8,128)(2,1)} fusion(f32[1024,768]{0,1:T(8,128)} %get-tuple-element.128, bf16[3072,768]{1,0:T(8,128)(2,1)} %all-gather.11.cloned.1.call-done, f32[768]{0:T(1024)S(1)} %convert_element_type.149, f32[1024,3072]{1,0:T(8,128)} %fusion.68, f32[3072]{0:T(1024)S(1)} %copy-done.44), kind=kOutput, calls=%fused_computation.69 | convolution fusion | flops 4866441216 | bytes 22035456 | tf_op jit(solution)/shard_map/dot_general | solution.py:28
  452.0 9.2 %fusion.77 = (f32[768]{0:T(1024)S(1)}, f32[1024,768]{1,0:T(8,128)}) fusion(bf16[768,2304]{1,0:T(8,128)(2,1)} %all-gather.5.cloned.1.call-done, bf16[1024,768]{0,1:T(8,128)(2,1)} %bitcast.89, bf16[1024,768]{0,1:T(8,128)(2,1)} %bitcast.79, bf16[1024,768]{0,1:T(8,128)(2,1)} %bitcast.84), kind=kOutput, calls=%fused_computation.130 | convolution fusion | flops 3638820096 | bytes 11406336 | tf_op jit(solution)/shard_map/dot_general | solution.py:38
  470.2 41.3 %all-reduce.18 = (f32[768]{0:T(1024)S(1)}, f32[768]{0:T(1024)S(1)}, f32[1536]{0:T(1024)S(1)}, f32[768]{0:T(1024)S(1)}, f32[768]{0:T(1024)S(1)}, /*index=5*/f32[7...) all-reduce(f32[768]{0:T(1024)S(1)} %get-tuple-element.88, ...), channel_id=2, replica_groups=mesh['wide'=8,'narrow'=4] {'wide','narrow'}, use_global_device_ids=true, to_apply=%region_15.16.clone | all-reduce | flops 9216 | bytes 73728
  515.1 5.7 add_convert_fusion.1
  524.5 17.9 %reduce-scatter.5.cloned.1.call-done = f32[24,2304]{1,0:T(8,128)} async-done(((f32[768,2304]{1,0:T(8,128)}), f32[24,2304]{1,0:T(8,128)}) %reduce-scatter.5.cloned.1.call-update) | async-done | bytes 221200 | tf_op jit(solution)/shard_map/reduce_scatter | solution.py:289
  542.5 141.2 %reduce-scatter.11.cloned.1.call-done = f32[96,768]{1,0:T(8,128)} async-done(((f32[3072,768]{1,0:T(8,128)}), f32[96,768]{1,0:T(8,128)}) %reduce-scatter.11.cloned.1.call-update) | async-done | bytes 294928 | tf_op jit(solution)/shard_map/reduce_scatter | solution.py:255
  683.7 142.0 %reduce-scatter.9.cloned.1.call-done = f32[24,3072]{1,0:T(8,128)} async-done(((f32[768,3072]{1,0:T(8,128)}), f32[24,3072]{1,0:T(8,128)}) %reduce-scatter.9.cloned.1.call-update) | async-done | bytes 294928 | tf_op jit(solution)/shard_map/reduce_scatter | solution.py:253
  (233 shorter events, 93.1 us)
Async XLA Ops:
  7.2 66.9 %all-gather.5.cloned.1.call-start = ((), (), s32[]{:S(2)}) async-start(), calls=%async_computation.4 | async-start | bytes 3649536 | tf_op jit(solution)/shard_map/all_gather | solution.py:182
  7.9 146.8 %all-gather.7.cloned.1.call-start = ((), (), s32[]{:S(2)}) async-start(), calls=%async_computation.5 | async-start | bytes 1216512 | tf_op jit(solution)/shard_map/all_gather | solution.py:184
  8.7 186.7 %all-gather.9.cloned.1.call-start = ((), (), s32[]{:S(2)}) async-start(), calls=%async_computation.6 | async-start | bytes 4866048 | tf_op jit(solution)/shard_map/all_gather | solution.py:213
  9.4 251.2 %all-gather.11.cloned.1.call-start = ((), (), s32[]{:S(2)}) async-start(), calls=%async_computation.7 | async-start | bytes 4866048 | tf_op jit(solution)/shard_map/all_gather | solution.py:215
  10.0 514.5 %reduce-scatter.7.cloned.1.call-start = ((), (), s32[]{:S(2)}) async-start(), calls=%async_computation.9 | async-start | bytes 2433024 | tf_op jit(solution)/shard_map/reduce_scatter | solution.py:291
  62.1 12.1 %copy-start.29 = (f32[768]{0:T(1024)}, f32[768]{0:T(1024)S(1)}, u32[]{:S(2)}) copy-start(f32[768]{0:T(1024)S(1)} %convert_element_type.133) | copy-start | bytes 9220
  62.1 12.1 %copy-start.46 = (f32[768]{0:T(1024)}, f32[768]{0:T(1024)S(1)}, u32[]{:S(2)}) copy-start(f32[768]{0:T(1024)S(1)} %convert_element_type.134) | copy-start | bytes 9220
  62.1 133.3 %copy-start.24 = (f32[768]{0:T(1024)}, f32[768]{0:T(1024)S(1)}, u32[]{:S(2)}) copy-start(f32[768]{0:T(1024)S(1)} %convert_element_type.145) | copy-start | bytes 9220
  65.6 89.1 %copy-start.2 = (bf16[1024,768]{0,1:T(8,128)(2,1)}, bf16[1024,768]{0,1:T(8,128)(2,1)S(1)}, u32[]{:S(2)}) copy-start(bf16[1024,768]{0,1:T(8,128)(2,1)S(1)} %copy.73) | copy-start | bytes 4718596
  65.9 14.6 %copy-start.27 = (f32[1024]{0:T(1024)}, f32[1024]{0:T(1024)S(1)}, u32[]{:S(2)}) copy-start(f32[1024]{0:T(1024)S(1)} %broadcast_multiply_fusion.1) | copy-start | bytes 12292
  66.9 13.6 %copy-start.33 = (f32[1024]{0:T(1024)}, f32[1024]{0:T(1024)S(1)}, u32[]{:S(2)}) copy-start(f32[1024]{0:T(1024)S(1)} %fusion.46) | copy-start | bytes 12292
  68.7 191.9 %copy-start.6 = (bf16[1024,768]{0,1:T(8,128)(2,1)}, bf16[1024,768]{0,1:T(8,128)(2,1)S(1)}, u32[]{:S(2)}) copy-start(bf16[1024,768]{0,1:T(8,128)(2,1)S(1)} %copy.82) | copy-start | bytes 4718596
  106.8 14.6 %copy-start.11 = (pred[512,1024]{1,0:T(8,128)(4,1)S(1)}, pred[512,1024]{1,0:T(8,128)(4,1)}, u32[]{:S(2)}) copy-start(pred[512,1024]{1,0:T(8,128)(4,1)} %iota_compare_fusion) | copy-start | bytes 1572868
  121.4 13.4 %copy-start.20 = (bf16[512,768]{0,1:T(8,128)(2,1)S(1)}, bf16[512,768]{0,1:T(8,128)(2,1)}, u32[]{:S(2)}) copy-start(bf16[512,768]{0,1:T(8,128)(2,1)} %copy.74) | copy-start | bytes 2359300
  121.4 21.6 %slice-start = ((s8[25165824]{0:T(1024)(128)(4,1)}), s8[4194304]{0:T(1024)(128)(4,1)S(1)}, s32[]{:S(2)}) async-start(s8[25165824]{0:T(1024)(128)(4,1)} %bitcast.68), calls=%async_computation.12 | async-start | bytes 8388608
  121.4 21.6 %slice-start.1 = ((s8[25165824]{0:T(1024)(128)(4,1)}), s8[4194304]{0:T(1024)(128)(4,1)S(1)}, s32[]{:S(2)}) async-start(s8[25165824]{0:T(1024)(128)(4,1)} %bitcast.68), calls=%async_computation.13 | async-start | bytes 8388608
  163.2 97.4 %copy-start.32 = (f32[1024]{0:T(1024)S(1)}, f32[1024]{0:T(1024)}, u32[]{:S(2)}) copy-start(f32[1024]{0:T(1024)} %fusion.45) | copy-start | bytes 12292
  163.2 97.4 %copy-start.44 = (f32[3072]{0:T(1024)S(1)}, f32[3072]{0:T(1024)}, u32[]{:S(2)}) copy-start(f32[3072]{0:T(1024)} %convert_element_type.147) | copy-start | bytes 36868
  260.6 18.6 %copy-start.16 = (bf16[768,3072]{1,0:T(8,128)(2,1)S(1)}, bf16[768,3072]{1,0:T(8,128)(2,1)}, u32[]{:S(2)}) copy-start(bf16[768,3072]{1,0:T(8,128)(2,1)} %all-gather.9.cloned.1.call-done) | copy-start | bytes 14155780
  302.8 28.7 %copy-start.22 = (bf16[512,768]{0,1:T(8,128)(2,1)}, bf16[512,768]{0,1:T(8,128)(2,1)S(1)}, u32[]{:S(2)}) copy-start(bf16[512,768]{0,1:T(8,128)(2,1)S(1)} %get-tuple-element.117) | copy-start | bytes 2359300
  317.8 224.7 %reduce-scatter.5.cloned.1.call-start = ((), (), s32[]{:S(2)}) async-start(), calls=%async_computation.8 | async-start | bytes 7299072 | tf_op jit(solution)/shard_map/reduce_scatter | solution.py:289
  317.8 10.2 %copy-start.14 = (bf16[512,768]{0,1:T(8,128)(2,1)S(1)}, bf16[512,768]{0,1:T(8,128)(2,1)}, u32[]{:S(2)}) copy-start(bf16[512,768]{0,1:T(8,128)(2,1)} %copy.75) | copy-start | bytes 2359300
  382.0 19.3 %copy-start.10 = (bf16[1024,12,64]{0,2,1:T(8,128)(2,1)}, bf16[1024,12,64]{0,2,1:T(8,128)(2,1)S(1)}, u32[]{:S(2)}) copy-start(bf16[1024,12,64]{0,2,1:T(8,128)(2,1)S(1)} %fusion.31) | copy-start | bytes 4718596
  388.5 12.8 %copy-start.15 = (bf16[1024,12,64]{0,2,1:T(8,128)(2,1)}, bf16[1024,12,64]{0,2,1:T(8,128)(2,1)S(1)}, u32[]{:S(2)}) copy-start(bf16[1024,12,64]{0,2,1:T(8,128)(2,1)S(1)} %pad_maximum_fusion.1) | copy-start | bytes 4718596
  388.5 14.0 %copy-start.3 = (bf16[1024,768]{0,1:T(8,128)(2,1)S(1)}, bf16[1024,768]{0,1:T(8,128)(2,1)}, u32[]{:S(2)}) copy-start(bf16[1024,768]{0,1:T(8,128)(2,1)} %copy-done.2) | copy-start | bytes 4718596
  388.5 14.0 %copy-start.28 = (f32[1024]{0:T(1024)S(1)}, f32[1024]{0:T(1024)}, u32[]{:S(2)}) copy-start(f32[1024]{0:T(1024)} %copy-done.27) | copy-start | bytes 12292
  388.5 14.0 %copy-start.30 = (f32[768]{0:T(1024)S(1)}, f32[768]{0:T(1024)}, u32[]{:S(2)}) copy-start(f32[768]{0:T(1024)} %copy-done.29) | copy-start | bytes 9220
  388.5 14.0 %copy-start.34 = (f32[1024]{0:T(1024)S(1)}, f32[1024]{0:T(1024)}, u32[]{:S(2)}) copy-start(f32[1024]{0:T(1024)} %copy-done.33) | copy-start | bytes 12292
  388.5 14.0 %copy-start.47 = (f32[768]{0:T(1024)S(1)}, f32[768]{0:T(1024)}, u32[]{:S(2)}) copy-start(f32[768]{0:T(1024)} %copy-done.46) | copy-start | bytes 9220
  409.5 274.1 %reduce-scatter.11.cloned.1.call-start = ((), (), s32[]{:S(2)}) async-start(), calls=%async_computation.11 | async-start | bytes 9732096 | tf_op jit(solution)/shard_map/reduce_scatter | solution.py:255
  425.1 400.6 %reduce-scatter.9.cloned.1.call-start = ((), (), s32[]{:S(2)}) async-start(), calls=%async_computation.10 | async-start | bytes 9732096 | tf_op jit(solution)/shard_map/reduce_scatter | solution.py:253
  468.8 46.3 %copy-start.36 = (f32[1024]{0:T(1024)S(1)}, f32[1024]{0:T(1024)}, u32[]{:S(2)}) copy-start(f32[1024]{0:T(1024)} %copy-done.35) | copy-start | bytes 12292
  (42 other events, 161.7 us)
Sparse Core Ops, SparseCore 0:
  10.9 63.1 all-gather.4
  77.0 52.8 all-gather.6
  132.8 62.5 all-gather.8
  198.2 62.3 all-gather.10
  317.9 97.8 reduce-scatter.6
  422.8 119.5 reduce-scatter.4
  548.9 134.7 reduce-scatter.10
  691.2 134.4 reduce-scatter.8
where the time goes:
time: 840 us; the launch traced here: 833 us
  waiting for transfers between devices  396 us (47%)
  matrix products  210 us (25%)
  blocking collectives  84.1 us (10%)
  other arithmetic  70.2 us (8%)
  local copies, waits for them, and re-layouts  56.5 us (7%)
  between operations  15.9 us (2%)
    reduce_scatter x1, waiting for transfers between devices, local(): lax.psum_scatter(fc_weight_term, ('wide', 'narrow'), scatter_dimension=0,...  142 us
    reduce_scatter x1, waiting for transfers between devices, local(): lax.psum_scatter(proj_weight_term, ('wide', 'narrow'), scatter_dimension=...  141 us
    unnamed x2, blocking collectives  84.1 us
    all_gather x1, waiting for transfers between devices, local(): lax.all_gather(proj_weight, ('wide', 'narrow'), axis=0, tiled=True)  54.2 us
    dot_general x4, matrix products, right_product(): lax.dot_general(left, right, (((1,), (1,)), ((), ())), preferred_element_...  36.6 us
    dot_general x4, matrix products, product(): return jnp.dot(left, right, preferred_element_type=jnp.float32)  35.3 us
    dot_general x4, matrix products, left_product(): lax.dot_general(left, right, (((0,), (0,)), ((), ())), preferred_element_...  34.7 us
    all_gather x1, waiting for transfers between devices, local(): lax.all_gather(fc_weight, ('wide', 'narrow'), axis=0, tiled=True)  32.1 us
  transfers between devices with their start and end apart: 8, of which 6 were waited for; matrix products, arithmetic and copies ran while one was open for 32% of the time, Pallas kernels for 0%

commit v1 on v0

--- a/solution.py
+++ b/solution.py
@@ -1,3 +1,4 @@
+import functools
 import math
 import jax
 import jax.numpy as jnp
@@ -10,6 +11,23 @@
 branch_scale = 1.0 / math.sqrt(48.0)
 norm_epsilon = 1e-05
 masked_value = -1e30
+
+
+def attach_units(obj, group_axis):
+    arr_next = lax.axis_size(group_axis)
+    tmp = lax.axis_index(group_axis)
+    r2, wide_out = (arr_next, tmp)
+    moved, newest = (obj, 1)
+    while newest < r2:
+        view_out = lax.ppermute(moved, group_axis, [(tick, tick ^ newest) for tick in range(r2)])
+        carry = jnp.concatenate([moved, view_out], axis=0)
+        tall = jnp.concatenate([view_out, moved], axis=0)
+        moved = jnp.where(wide_out & newest == 0, carry, tall)
+        newest = 2 * newest
+    return moved
+
+
+_enter_marks = functools.partial(attach_units, group_axis=("wide", "narrow"))
 
 
 def layer_norm(values_in, gain_vec, shift_vec):
@@ -210,7 +228,7 @@
     mlp_full = (
         lax.all_gather(norm2_gain, ("wide", "narrow"), axis=0, tiled=True),
         lax.all_gather(norm2_bias, ("wide", "narrow"), axis=0, tiled=True),
-        lax.all_gather(fc_weight, ("wide", "narrow"), axis=0, tiled=True),
+        _enter_marks(fc_weight),
         lax.all_gather(fc_bias, ("wide", "narrow"), axis=0, tiled=True),
         lax.all_gather(proj_weight, ("wide", "narrow"), axis=0, tiled=True),
         lax.all_gather(proj_bias, ("wide", "narrow"), axis=0, tiled=True),

time: 840 us -> 914 us (1.088)
  waiting for transfers between devices: 396 us -> 456 us
    ppermute x0 -> x5, waiting for transfers between devices: none -> 34.6 us  [attach_units(): lax.ppermute(moved, group_axis, [(tick, tick ^ newest) for tick in range(...]
    all_gather x1, waiting for transfers between devices: 0.01 us -> 26.8 us  [local(): lax.all_gather(out_weight, ('wide', 'narrow'), axis=0, tiled=True)]
    all_gather x1, waiting for transfers between devices: 32.1 us -> 44.9 us  [local(): lax.all_gather(fc_weight, ('wide', 'narrow'), axis=0, tiled=True)]
    all_gather x1, waiting for transfers between devices: 54.2 us -> 44.9 us  [local(): lax.all_gather(proj_weight, ('wide', 'narrow'), axis=0, tiled=True)]
    unnamed x160 -> x148, local copies, waits for them, and re-layouts: 32 us -> 30.7 us
  transfers between devices with their start and end apart: 8 -> 13, of which waited for: 6 -> 9; matrix products, arithmetic and copies ran while one was open for 32% -> 32% of each run, Pallas kernels for 0% -> 0%
where the time goes in v1:
time: 914 us; the launch traced here: 906 us
  waiting for transfers between devices  456 us (50%)
  matrix products  216 us (24%)
  blocking collectives  82.6 us (9%)
  other arithmetic  71.5 us (8%)
  local copies, waits for them, and re-layouts  56.4 us (6%)
  between operations  15.9 us (2%)
    reduce_scatter x1, waiting for transfers between devices, local(): lax.psum_scatter(fc_weight_term, ('wide', 'narrow'), scatter_dimension=0,...  142 us
    reduce_scatter x1, waiting for transfers between devices, local(): lax.psum_scatter(proj_weight_term, ('wide', 'narrow'), scatter_dimension=...  141 us
    unnamed x2, blocking collectives  82.6 us
    all_gather x1, waiting for transfers between devices, local(): lax.all_gather(fc_weight, ('wide', 'narrow'), axis=0, tiled=True)  44.9 us
    all_gather x1, waiting for transfers between devices, local(): lax.all_gather(proj_weight, ('wide', 'narrow'), axis=0, tiled=True)  44.9 us
    dot_general x4, matrix products, right_product(): lax.dot_general(left, right, (((1,), (1,)), ((), ())), preferred_element_...  41.3 us
    dot_general x4, matrix products, product(): return jnp.dot(left, right, preferred_element_type=jnp.float32)  36.5 us
    dot_general x4, matrix products, left_product(): lax.dot_general(left, right, (((0,), (0,)), ((), ())), preferred_element_...  34.6 us
  transfers between devices with their start and end apart: 13, of which 9 were waited for; matrix products, arithmetic and copies ran while one was open for 32% of the time, Pallas kernels for 0%

profile of v1, /device:TPU:0, one launch (start us, length us, event | category | flops | bytes accessed | tf_op | source)
XLA Modules:
  0.0 905.9 jit_solution(2582523267955321520)
XLA Ops:
  15.3 7.2 collective-permute-done.1
  32.5 41.1 %all-reduce.19 = (bf16[768]{0:T(1024)(128)(2,1)S(1)}, bf16[1536]{0:T(1024)(128)(2,1)S(1)}, bf16[768]{0:T(1024)(128)(2,1)S(1)}, bf16[768]{0:T(1024)(128)(2,1)S(1)...) all-reduce(bf16[768]{0:T(1024)(128)(2,1)S(1)} %dynamic-update-slice, ...), channel_id=1, replica_groups=mesh['wide'=8,'narrow'=4] {'wide','narrow'}, use_global_device_ids=true, to_apply=%add.5 | all-reduce | flops 9216 | bytes 36864
  83.9 26.1 %collective-permute-done.3 = bf16[192,3072]{1,0:T(8,128)(2,1)S(1)} collective-permute-done((bf16[192,3072]{1,0:T(8,128)(2,1)S(1)}, bf16[192,3072]{1,0:T(8,128)(2,1)S(1)}, u32[]{:S(2)}, u32[]{:S(2)}) %collective-permute-start.3) | collective-permute-done | bytes 1179680 | tf_op jit(solution)/shard_map/ppermute | solution.py:22
  113.4 6.4 add_convert_fusion
  146.1 14.4 %fusion.2 = (f32[12,512]{1,0:T(8,128)S(1)}, f32[12,512,1024]{2,1,0:T(8,128)}) fusion(pred[512,1024]{1,0:T(8,128)(4,1)} %iota_compare_fusion, bf16[512,12,64]{0,2,1:T(8,128)(2,1)} %bitcast.73, bf16[1024,12,64]{0,2,1:T(8,128)(2,1)} %bitcast.69), kind=kOutput, calls=%fused_computation.11 | convolution fusion | flops 824174592 | bytes 28073984 | tf_op jit(solution)/shard_map/while/body/eval_jaxpr/qhd,khd->hqk/dot_general | solution.py:72
  160.5 12.4 %fusion = f32[12,512]{1,0:T(8,128)S(1)} fusion(f32[12,512,1024]{2,1,0:T(8,128)} %get-tuple-element.124, f32[12,512]{1,0:T(8,128)S(1)} %get-tuple-element.123, pred[512,1024]{1,0:T(8,128)(4,1)S(1)} %copy-done.15), kind=kLoop, calls=%fused_computation.6 | loop fusion | flops 25159680 | bytes 25739264 | tf_op jit(solution)/shard_map/while/body/eval_jaxpr/reduce_sum | solution.py:85
  176.0 9.9 %fusion.12 = f32[12,64,512]{2,1,0:T(8,128)} fusion(bf16[1024,12,64]{0,2,1:T(8,128)(2,1)} %bitcast.83, f32[12,512,1024]{2,1,0:T(8,128)S(1)} %copy-done, f32[12,512]{1,0:T(8,128)S(1)} %fusion, f32[12,512]{1,0:T(8,128)S(1)} %get-tuple-element.123, pred[512,1024]{1,0:T(8,128)(4,1)S(1)} %copy-done.15), kind=kOutput, calls=%fused_computation.29 | convolution fusion | flops 836763648 | bytes 28884992 | tf_op jit(solution)/shard_map/while/body/eval_jaxpr/hqk,khd->qhd/dot_general | solution.py:87
  185.8 7.7 fusion.17
  193.6 26.8 %all-gather.7.cloned.1.call-done = bf16[768,768]{1,0:T(8,128)(2,1)} async-done(((bf16[24,768]{1,0:T(8,128)(2,1)}), bf16[768,768]{1,0:T(8,128)(2,1)}) %all-gather.7.cloned.1.call-update) | async-done | bytes 1179664 | tf_op jit(solution)/shard_map/all_gather | solution.py:202
  226.1 13.8 %fusion.22 = f32[1024,3072]{1,0:T(8,128)} fusion(bf16[384,3072]{1,0:T(8,128)(2,1)} %collective-permute-done.4, bf16[384,3072]{1,0:T(8,128)(2,1)} %maximum_select_fusion.2, pred[]{:T(512)S(6)} %eq.15, f32[1024,768]{0,1:T(8,128)S(1)} %get-tuple-element.128, f32[768]{0:T(1024)S(1)} %copy-done.46, f32[768]{0:T(1024)S(1)} %convert_element_type.144, ...), kind=kOutput, calls=%fused_computation.47 | convolution fusion | flops 4857004032 | bytes 20461568 | tf_op jit(solution)/shard_map/dot_general | solution.py:46
  239.9 44.9 %all-gather.9.cloned.1.call-done = bf16[3072,768]{1,0:T(8,128)(2,1)} async-done(((bf16[96,768]{1,0:T(8,128)(2,1)}), bf16[3072,768]{1,0:T(8,128)(2,1)}) %all-gather.9.cloned.1.call-update) | async-done | bytes 4718608 | tf_op jit(solution)/shard_map/all_gather | solution.py:233
  284.7 20.3 %convert_reduce_fusion = (f32[3072]{0:T(1024)}, bf16[1024,3072]{1,0:T(8,128)(2,1)}) fusion(f32[1024,3072]{1,0:T(8,128)} %fusion.22, f32[3072]{0:T(1024)S(1)} %copy-done.44, bf16[3072,768]{1,0:T(8,128)(2,1)} %all-gather.9.cloned.1.call-done, bf16[1024,768]{0,1:T(8,128)(2,1)S(1)} %copy.82, f32[1024]{0:T(1024)S(1)} %fusion.52), kind=kOutput, calls=%fused_computation.18 | convolution fusion | flops 4919915520 | bytes 25194496 | tf_op jit(solution)/shard_map/dot_general | solution.py:56
  305.0 44.9 %all-gather.11.cloned.1.call-done = bf16[768,3072]{1,0:T(8,128)(2,1)} async-done(((bf16[24,3072]{1,0:T(8,128)(2,1)}), bf16[768,3072]{1,0:T(8,128)(2,1)}) %all-gather.11.cloned.1.call-update) | async-done | bytes 4718608 | tf_op jit(solution)/shard_map/all_gather | solution.py:248
  349.9 10.4 %fusion.85 = (f32[768]{0:T(1024)}, f32[1024,768]{1,0:T(8,128)}) fusion(bf16[1024,3072]{1,0:T(8,128)(2,1)} %get-tuple-element.138, bf16[768,3072]{1,0:T(8,128)(2,1)} %all-gather.11.cloned.1.call-done), kind=kOutput, calls=%fused_computation.143 | convolution fusion | flops 4832623616 | bytes 14158848 | tf_op jit(solution)/shard_map/dot_general | solution.py:56
  375.9 8.1 fusion.42
  384.1 7.0 multiply_reduce_fusion.1
  391.2 10.0 %multiply_convert_fusion.1 = bf16[12,512,512]{1,2,0:T(8,128)(2,1)S(1)} fusion(f32[12,512,512]{1,2,0:T(8,128)} %get-tuple-element.130, f32[12,512]{1,0:T(8,128)S(1)} %get-tuple-element.129, f32[12,512]{1,0:T(8,128)S(1)} %copy-done.28, f32[12,512,512]{1,2,0:T(8,128)} %copy-done.1, pred[512,512]{0,1:T(8,128)(4,1)S(1)} %iota_compare_fusion.1), kind=kLoop, calls=%fused_computation.21 | loop fusion | flops 22020096 | bytes 31768576 | tf_op jit(solution)/shard_map/while/body/eval_jaxpr/convert_element_type | solution.py:149
  404.6 22.1 %multiply_reduce_fusion = (f32[12,512]{1,0:T(8,128)S(1)}, f32[12,512,1024]{2,1,0:T(8,128)}) fusion(f32[12,512]{1,0:T(8,128)S(1)} %log_add_fusion, f32[12,512,1024]{2,1,0:T(8,128)} %get-tuple-element.124, pred[512,1024]{1,0:T(8,128)(4,1)S(1)} %copy-done.16, bf16[512,12,64]{0,2,1:T(8,128)(2,1)S(1)} %bitcast.90, bf16[1024,12,64]{0,2,1:T(8,128)(2,1)S(1)} %bitcast.84), kind=kOutput, calls=%fused_computation.1 | convolution fusion | flops 843048960 | bytes 53264384 | tf_op jit(solution)/shard_map/while/body/eval_jaxpr/qhd,khd->hqk/dot_general | solution.py:145
  426.8 18.1 %multiply_convert_fusion = bf16[12,512,1024]{2,1,0:T(8,128)(2,1)S(1)} fusion(f32[12,512,1024]{2,1,0:T(8,128)} %get-tuple-element.132, f32[12,512]{1,0:T(8,128)S(1)} %get-tuple-element.131, f32[12,512]{1,0:T(8,128)S(1)} %log_add_fusion, f32[12,512,1024]{2,1,0:T(8,128)} %get-tuple-element.124, pred[512,1024]{1,0:T(8,128)(4,1)} %iota_compare_fusion), kind=kLoop, calls=%fused_computation | loop fusion | flops 44040192 | bytes 63488000 | tf_op jit(solution)/shard_map/while/body/eval_jaxpr/convert_element_type | solution.py:149
  444.9 6.2 fusion.45
  455.2 4.6 fusion.46
  460.1 12.8 %fusion.37 = bf16[1024,12,64]{0,2,1:T(8,128)(2,1)S(1)} fusion(f32[512,12,64]{0,2,1:T(8,128)S(1)} %copy-done.56, bf16[512,12,64]{0,2,1:T(8,128)(2,1)S(1)} %bitcast.91, f32[12,512]{1,0:T(8,128)S(1)} %log_add_fusion, f32[12,512,1024]{2,1,0:T(8,128)} %get-tuple-element.124, pred[512,1024]{1,0:T(8,128)(4,1)S(1)} %copy-done.17), kind=kOutput, calls=%fused_computation.65 | convolution fusion | flops 838336512 | bytes 29646848 | tf_op jit(solution)/shard_map/while/body/eval_jaxpr/hqk,qhd->khd/dot_general | solution.py:142
  474.1 7.0 fusion.71
  482.5 14.0 %fusion.47 = f32[3072,768]{1,0:T(8,128)} fusion(bf16[1024,768]{0,1:T(8,128)(2,1)S(1)} %copy-done.12, f32[1024]{0:T(1024)S(1)} %fusion.52, f32[1024,3072]{1,0:T(8,128)} %fusion.22, f32[3072]{0:T(1024)S(1)} %copy-done.44), kind=kOutput, calls=%fused_computation.93 | convolution fusion | flops 4866441216 | bytes 23609344 | tf_op jit(solution)/shard_map/dot_general | solution.py:50
  497.2 10.7 %fusion.75 = f32[768,3072]{1,0:T(8,128)} fusion(bf16[1024,3072]{1,0:T(8,128)(2,1)} %get-tuple-element.138, f32[1024,768]{0,1:T(8,128)} %copy-done.7, f32[768]{0:T(1024)S(1)} %copy-done.47, f32[768]{0:T(1024)S(1)} %convert_element_type.144, f32[1024]{0:T(1024)S(1)} %copy-done.40, f32[1024]{0:T(1024)S(1)} %broadcast_multiply_fusion), kind=kOutput, calls=%fused_computation.135 | convolution fusion | flops 4835770368 | bytes 18888704 | tf_op jit(solution)/shard_map/dot_general | solution.py:50
  508.6 12.4 %add_convert_fusion.2 = bf16[1024,768]{0,1:T(8,128)(2,1)} fusion(f32[1024,768]{0,1:T(8,128)} %copy-done.7, bf16[3072,768]{1,0:T(8,128)(2,1)} %all-gather.9.cloned.1.call-done, f32[768]{0:T(1024)S(1)} %convert_element_type.149, f32[1024,3072]{1,0:T(8,128)} %fusion.22, f32[3072]{0:T(1024)S(1)} %copy-done.44), kind=kOutput, calls=%fused_computation.77 | convolution fusion | flops 4866441216 | bytes 22035456 | tf_op jit(solution)/shard_map/dot_general | solution.py:46
  523.5 9.2 %fusion.84 = (f32[768]{0:T(1024)S(1)}, f32[1024,768]{1,0:T(8,128)}) fusion(bf16[768,2304]{1,0:T(8,128)(2,1)} %all-gather.5.cloned.1.call-done, bf16[1024,768]{0,1:T(8,128)(2,1)} %bitcast.86, bf16[1024,768]{0,1:T(8,128)(2,1)} %bitcast.76, bf16[1024,768]{0,1:T(8,128)(2,1)} %bitcast.81), kind=kOutput, calls=%fused_computation.142 | convolution fusion | flops 3638820096 | bytes 11406336 | tf_op jit(solution)/shard_map/dot_general | solution.py:56
  541.8 41.5 %all-reduce.18 = (f32[768]{0:T(1024)S(1)}, f32[768]{0:T(1024)S(1)}, f32[1536]{0:T(1024)S(1)}, f32[768]{0:T(1024)S(1)}, f32[768]{0:T(1024)S(1)}, /*index=5*/f32[7...) all-reduce(f32[768]{0:T(1024)S(1)} %get-tuple-element.88, ...), channel_id=2, replica_groups=mesh['wide'=8,'narrow'=4] {'wide','narrow'}, use_global_device_ids=true, to_apply=%region_15.16.clone | all-reduce | flops 9216 | bytes 73728
  586.8 5.6 add_convert_fusion.1
  596.1 19.3 %reduce-scatter.5.cloned.1.call-done = f32[24,2304]{1,0:T(8,128)} async-done(((f32[768,2304]{1,0:T(8,128)}), f32[24,2304]{1,0:T(8,128)}) %reduce-scatter.5.cloned.1.call-update) | async-done | bytes 221200 | tf_op jit(solution)/shard_map/reduce_scatter | solution.py:307
  615.4 141.2 %reduce-scatter.11.cloned.1.call-done = f32[96,768]{1,0:T(8,128)} async-done(((f32[3072,768]{1,0:T(8,128)}), f32[96,768]{1,0:T(8,128)}) %reduce-scatter.11.cloned.1.call-update) | async-done | bytes 294928 | tf_op jit(solution)/shard_map/reduce_scatter | solution.py:273
  756.7 142.1 %reduce-scatter.9.cloned.1.call-done = f32[24,3072]{1,0:T(8,128)} async-done(((f32[768,3072]{1,0:T(8,128)}), f32[24,3072]{1,0:T(8,128)}) %reduce-scatter.9.cloned.1.call-update) | async-done | bytes 294928 | tf_op jit(solution)/shard_map/reduce_scatter | solution.py:271
  (234 shorter events, 111.8 us)
Async XLA Ops:
  7.2 67.7 %copy-start.21 = (bf16[1024,768]{1,0:T(8,128)(2,1)S(1)}, bf16[1024,768]{1,0:T(8,128)(2,1)}, u32[]{:S(2)}) copy-start(bf16[1024,768]{1,0:T(8,128)(2,1)} %param.15) | copy-start | bytes 4718596
  7.2 106.2 %all-gather.5.cloned.1.call-start = ((), (), s32[]{:S(2)}) async-start(), calls=%async_computation.4 | async-start | bytes 3649536 | tf_op jit(solution)/shard_map/all_gather | solution.py:200
  7.9 212.5 %all-gather.7.cloned.1.call-start = ((), (), s32[]{:S(2)}) async-start(), calls=%async_computation.5 | async-start | bytes 1216512 | tf_op jit(solution)/shard_map/all_gather | solution.py:202
  8.7 276.0 %all-gather.9.cloned.1.call-start = ((), (), s32[]{:S(2)}) async-start(), calls=%async_computation.6 | async-start | bytes 4866048 | tf_op jit(solution)/shard_map/all_gather | solution.py:233
  9.4 340.5 %all-gather.11.cloned.1.call-start = ((), (), s32[]{:S(2)}) async-start(), calls=%async_computation.7 | async-start | bytes 4866048 | tf_op jit(solution)/shard_map/all_gather | solution.py:248
  9.5 1.7 collective-permute-start
  12.2 10.3 %collective-permute-start.1 = (bf16[48,3072]{1,0:T(8,128)(2,1)S(1)}, bf16[48,3072]{1,0:T(8,128)(2,1)S(1)}, u32[]{:S(2)}, u32[]{:S(2)}) collective-permute-start(bf16[48,3072]{1,0:T(8,128)(2,1)S(1)} %maximum_select_fusion.5), channel_id=1, source_target_pairs={{0,2},{1,3},{2,0},{3,1},{4,6},{5,7},{6,4},{7,5},{8,10},{9,11},{10,... | collective-permute-start | bytes 884744 | tf_op jit(solution)/shard_map/ppermute | solution.py:22
  15.2 580.9 %reduce-scatter.7.cloned.1.call-start = ((), (), s32[]{:S(2)}) async-start(), calls=%async_computation.9 | async-start | bytes 2433024 | tf_op jit(solution)/shard_map/reduce_scatter | solution.py:309
  23.4 54.6 %collective-permute-start.2 = (bf16[96,3072]{1,0:T(8,128)(2,1)}, bf16[96,3072]{1,0:T(8,128)(2,1)}, u32[]{:S(2)}, u32[]{:S(2)}) collective-permute-start(bf16[96,3072]{1,0:T(8,128)(2,1)} %maximum_select_fusion.4), channel_id=1, source_target_pairs={{0,4},{1,5},{2,6},{3,7},{4,0},{5,1},{6,2},{7,3},{8,12},{9,13},{10,... | collective-permute-start | bytes 1769480 | tf_op jit(solution)/shard_map/ppermute | solution.py:22
  73.6 39.8 %copy-start.31 = (f32[768]{0:T(1024)}, f32[768]{0:T(1024)S(1)}, u32[]{:S(2)}) copy-start(f32[768]{0:T(1024)S(1)} %convert_element_type.133) | copy-start | bytes 9220
  73.6 39.7 %copy-start.48 = (f32[768]{0:T(1024)}, f32[768]{0:T(1024)S(1)}, u32[]{:S(2)}) copy-start(f32[768]{0:T(1024)S(1)} %convert_element_type.134) | copy-start | bytes 9220
  75.6 144.8 %copy-start.3 = (bf16[1024,768]{0,1:T(8,128)(2,1)}, bf16[1024,768]{0,1:T(8,128)(2,1)S(1)}, u32[]{:S(2)}) copy-start(bf16[1024,768]{0,1:T(8,128)(2,1)S(1)} %copy.73) | copy-start | bytes 4718596
  77.9 206.8 %copy-start.10 = (bf16[1024,768]{0,1:T(8,128)(2,1)}, bf16[1024,768]{0,1:T(8,128)(2,1)S(1)}, u32[]{:S(2)}) copy-start(bf16[1024,768]{0,1:T(8,128)(2,1)S(1)} %copy.82) | copy-start | bytes 4718596
  80.5 29.5 %collective-permute-start.3 = (bf16[192,3072]{1,0:T(8,128)(2,1)S(1)}, bf16[192,3072]{1,0:T(8,128)(2,1)S(1)}, u32[]{:S(2)}, u32[]{:S(2)}) collective-permute-start(bf16[192,3072]{1,0:T(8,128)(2,1)S(1)} %maximum_select_fusion.3), channel_id=1, source_target_pairs={{0,8},{1,9},{2,10},{3,11},{4,12},{5,13},{6,14},{7,15},{8,0},{9,1},... | collective-permute-start | bytes 3538952 | tf_op jit(solution)/shard_map/ppermute | solution.py:22
  82.3 31.1 %copy-start.29 = (f32[1024]{0:T(1024)}, f32[1024]{0:T(1024)S(1)}, u32[]{:S(2)}) copy-start(f32[1024]{0:T(1024)S(1)} %broadcast_multiply_fusion.1) | copy-start | bytes 12292
  82.7 37.1 %copy-start.37 = (f32[1024]{0:T(1024)}, f32[1024]{0:T(1024)S(1)}, u32[]{:S(2)}) copy-start(f32[1024]{0:T(1024)S(1)} %fusion.34) | copy-start | bytes 12292
  82.7 37.1 %copy-start.33 = (f32[1024]{0:T(1024)}, f32[1024]{0:T(1024)S(1)}, u32[]{:S(2)}) copy-start(f32[1024]{0:T(1024)S(1)} %fusion.53) | copy-start | bytes 12292
  111.9 113.9 %collective-permute-start.4 = (bf16[384,3072]{1,0:T(8,128)(2,1)}, bf16[384,3072]{1,0:T(8,128)(2,1)}, u32[]{:S(2)}, u32[]{:S(2)}) collective-permute-start(bf16[384,3072]{1,0:T(8,128)(2,1)} %maximum_select_fusion.2), channel_id=1, source_target_pairs={{0,16},{1,17},{2,18},{3,19},{4,20},{5,21},{6,22},{7,23},{8,24},{9,... | collective-permute-start | bytes 7077896 | tf_op jit(solution)/shard_map/ppermute | solution.py:22
  146.1 14.4 %copy-start.15 = (pred[512,1024]{1,0:T(8,128)(4,1)S(1)}, pred[512,1024]{1,0:T(8,128)(4,1)}, u32[]{:S(2)}) copy-start(pred[512,1024]{1,0:T(8,128)(4,1)} %iota_compare_fusion) | copy-start | bytes 1572868
  160.5 15.5 %copy-start = (f32[12,512,1024]{2,1,0:T(8,128)S(1)}, f32[12,512,1024]{2,1,0:T(8,128)}, u32[]{:S(2)}) copy-start(f32[12,512,1024]{2,1,0:T(8,128)} %get-tuple-element.124) | copy-start | bytes 75497472
  225.9 58.9 %copy-start.44 = (f32[3072]{0:T(1024)S(1)}, f32[3072]{0:T(1024)}, u32[]{:S(2)}) copy-start(f32[3072]{0:T(1024)} %convert_element_type.147) | copy-start | bytes 36868
  375.9 28.7 %copy-start.26 = (bf16[512,768]{0,1:T(8,128)(2,1)}, bf16[512,768]{0,1:T(8,128)(2,1)S(1)}, u32[]{:S(2)}) copy-start(bf16[512,768]{0,1:T(8,128)(2,1)S(1)} %get-tuple-element.117) | copy-start | bytes 2359300
  391.1 224.3 %reduce-scatter.5.cloned.1.call-start = ((), (), s32[]{:S(2)}) async-start(), calls=%async_computation.8 | async-start | bytes 7299072 | tf_op jit(solution)/shard_map/reduce_scatter | solution.py:307
  455.2 17.7 %copy-start.14 = (bf16[1024,12,64]{0,2,1:T(8,128)(2,1)}, bf16[1024,12,64]{0,2,1:T(8,128)(2,1)S(1)}, u32[]{:S(2)}) copy-start(bf16[1024,12,64]{0,2,1:T(8,128)(2,1)S(1)} %fusion.38) | copy-start | bytes 4718596
  460.0 14.0 %copy-start.4 = (bf16[1024,768]{0,1:T(8,128)(2,1)S(1)}, bf16[1024,768]{0,1:T(8,128)(2,1)}, u32[]{:S(2)}) copy-start(bf16[1024,768]{0,1:T(8,128)(2,1)} %copy-done.3) | copy-start | bytes 4718596
  460.1 14.0 %copy-start.30 = (f32[1024]{0:T(1024)S(1)}, f32[1024]{0:T(1024)}, u32[]{:S(2)}) copy-start(f32[1024]{0:T(1024)} %copy-done.29) | copy-start | bytes 12292
  460.1 14.0 %copy-start.32 = (f32[768]{0:T(1024)S(1)}, f32[768]{0:T(1024)}, u32[]{:S(2)}) copy-start(f32[768]{0:T(1024)} %copy-done.31) | copy-start | bytes 9220
  460.1 14.0 %copy-start.34 = (f32[1024]{0:T(1024)S(1)}, f32[1024]{0:T(1024)}, u32[]{:S(2)}) copy-start(f32[1024]{0:T(1024)} %copy-done.33) | copy-start | bytes 12292
  460.1 14.0 %copy-start.49 = (f32[768]{0:T(1024)S(1)}, f32[768]{0:T(1024)}, u32[]{:S(2)}) copy-start(f32[768]{0:T(1024)} %copy-done.48) | copy-start | bytes 9220
  481.1 275.5 %reduce-scatter.11.cloned.1.call-start = ((), (), s32[]{:S(2)}) async-start(), calls=%async_computation.11 | async-start | bytes 9732096 | tf_op jit(solution)/shard_map/reduce_scatter | solution.py:273
  496.6 402.2 %reduce-scatter.9.cloned.1.call-start = ((), (), s32[]{:S(2)}) async-start(), calls=%async_computation.10 | async-start | bytes 9732096 | tf_op jit(solution)/shard_map/reduce_scatter | solution.py:271
  540.4 46.4 %copy-start.36 = (f32[1024]{0:T(1024)S(1)}, f32[1024]{0:T(1024)}, u32[]{:S(2)}) copy-start(f32[1024]{0:T(1024)} %copy-done.35) | copy-start | bytes 12292
  (41 other events, 153.4 us)
Sparse Core Ops, SparseCore 0:
  10.9 63.1 all-gather.4
  77.0 143.3 all-gather.6
  223.3 61.3 all-gather.8
  287.5 62.3 all-gather.10
  391.2 97.8 reduce-scatter.6
  496.1 119.2 reduce-scatter.4
  621.9 134.7 reduce-scatter.10
  764.2 134.5 reduce-scatter.8
